TPU v7x, 256 devices: a whole 4x4x8 slice. The times are simulated.
256 devices in a mesh: head: 16 (over x, y), qblk: 16 (over z, core).
Axes of the slice: x: 4, y: 4, z: 8, core: 2. Of those that a mesh axis runs over, the one named last changes fastest.
Arguments:
- queries: bfloat16 [32768, 4096], P(('qblk', 'head')), may hold values from -6 to 6
- key_states: bfloat16 [32768, 1024], P(('qblk', 'head')), may hold values from -6 to 6
- value_states: bfloat16 [32768, 1024], P(('qblk', 'head')), may hold values from -6 to 6
- vertical_blocks: int32 [32, 5], replicated, may hold values from 0 to 510, as said below
- slash_offsets: int32 [32, 8], replicated, may hold values from 1 to 64, as said below
Outputs:
- attended: bfloat16 [32768, 4096], P(('qblk', 'head'))
Inputs may be any that keep to these rules, and one draw needn't show every extreme that they name: `vertical_blocks`: each head names 5 distinct blocks, among them block 0 and block 510. `slash_offsets`: each head names 8 distinct offsets, among them 1 and 64.
All inputs are finite; a program needn't handle non-finite values.
Results may differ from a plain program's by a relative error of at most 0.0033.
Values may be sent and summed in bfloat16 or wider, within the bound.
No kernel may reach another device: no remote copies, remote signals or barrier semaphores. Data moves between devices by JAX's collectives and lax.ppermute only.
A program may use at most 64 MiB of HBM per device.

v0:
```python
import jax
import jax.numpy as jnp
from jax import lax
from jax.sharding import PartitionSpec as P

H = 32
KVH = 8
HD = 128
BLK = 64


def attend_group(
    query_block_list,
    diagonal_key_block,
    diagonal_value_block,
    slash_key_block,
    slash_value_block,
    vertical_key_block,
    vertical_value_block,
    block_ids,
    slash_row,
    vert_row,
):
    number_format = jnp.float32
    logit_scale = query_block_list.shape[-1] ** (-0.5)
    diagonal_scores = (
        jnp.einsum(
            "pwr,pgr->pwg",
            query_block_list,
            diagonal_key_block,
            preferred_element_type=number_format,
        )
        * logit_scale
    )
    slash_scores = (
        jnp.einsum(
            "pzf,opwf->pzow",
            query_block_list,
            slash_key_block,
            preferred_element_type=number_format,
        )
        * logit_scale
    )
    vertical_scores = (
        jnp.einsum(
            "ihx,zsx->ihzs",
            query_block_list,
            vertical_key_block,
            preferred_element_type=number_format,
        )
        * logit_scale
    )
    block_len = query_block_list.shape[1]
    causal = jnp.arange(block_len)[:, None] >= jnp.arange(block_len)[None, :]
    diagonal_scores = jnp.where(causal[None], diagonal_scores, -jnp.inf)
    slash_ok = block_ids[:, None] - slash_row[None, :] >= 0
    slash_scores = jnp.where(slash_ok[:, None, :, None], slash_scores, -jnp.inf)
    block_gap = block_ids[:, None] - vert_row[None, :]
    slash_hit = jnp.any(block_gap[:, :, None] == slash_row[None, None, :], axis=2)
    vert_ok = (block_gap > 0) & jnp.logical_not(slash_hit)
    vertical_scores = jnp.where(vert_ok[:, None, :, None], vertical_scores, -jnp.inf)
    row_max = jnp.maximum(
        jnp.max(diagonal_scores, axis=2),
        jnp.maximum(jnp.max(slash_scores, axis=(2, 3)), jnp.max(vertical_scores, axis=(2, 3))),
    )
    diagonal_weights = jnp.exp(diagonal_scores - row_max[:, :, None])
    slash_weights = jnp.exp(slash_scores - row_max[:, :, None, None])
    vertical_weights = jnp.exp(vertical_scores - row_max[:, :, None, None])
    row_total = (
        jnp.sum(diagonal_weights, axis=2)
        + jnp.sum(slash_weights, axis=(2, 3))
        + jnp.sum(vertical_weights, axis=(2, 3))
    )
    weight_total = jnp.einsum(
        "rmt,rtl->rml",
        diagonal_weights.astype(jnp.bfloat16),
        diagonal_value_block,
        preferred_element_type=number_format,
    )
    weight_total = weight_total + jnp.einsum(
        "mnop,ompj->mnj",
        slash_weights.astype(jnp.bfloat16),
        slash_value_block,
        preferred_element_type=number_format,
    )
    weight_total = weight_total + jnp.einsum(
        "tiyx,yxf->tif",
        vertical_weights.astype(jnp.bfloat16),
        vertical_value_block,
        preferred_element_type=number_format,
    )
    return (weight_total / row_total[:, :, None]).astype(jnp.bfloat16)


def take_rows(piece_rows, wanted, current):
    count = piece_rows.shape[1]
    inside = (wanted >= 0) & (wanted < count)
    picked = jnp.take(piece_rows, jnp.clip(wanted, 0, count - 1), axis=1)
    return jnp.where(inside[None, :, None, None], picked, current)


def take_vertical(piece_rows, wanted, kv_select, current):
    count = piece_rows.shape[1]
    inside = (wanted >= 0) & (wanted < count)
    picked = piece_rows[:, jnp.clip(wanted, 0, count - 1), kv_select[:, None]]
    return jnp.where(inside[None, :, :, None], picked, current)


def per_device(queries, key_states, value_states, vertical_blocks, slash_offsets):
    head_count = lax.axis_size("head")
    head_index = lax.axis_index("head")
    block_index = lax.axis_index("qblk")
    rows_in = queries.shape[0]
    q_heads = H // head_count
    copies = max(1, head_count // KVH)
    kv_heads = KVH * copies // head_count
    q_split = queries.reshape(1, rows_in, H, HD)
    kv_pair = jnp.stack([key_states, value_states], axis=0).reshape(2, rows_in, KVH, HD)
    kv_pair = jnp.repeat(kv_pair, copies, axis=2)
    q_local, kv_local = (
        lax.all_to_all(q_split, "head", split_axis=2, concat_axis=1, tiled=True),
        lax.all_to_all(kv_pair, "head", split_axis=2, concat_axis=1, tiled=True),
    )
    row_count = kv_local.shape[1]
    first_row = block_index * row_count
    vert_mine = lax.dynamic_slice_in_dim(vertical_blocks, head_index * q_heads, q_heads, 0)
    slash_mine = lax.dynamic_slice_in_dim(slash_offsets, head_index * q_heads, q_heads, 0)
    vert_count = vert_mine.shape[1]
    slash_count = slash_mine.shape[1]
    kv_select = jnp.arange(q_heads, dtype=jnp.int32) // (q_heads // kv_heads)
    want_vert = (
        vert_mine[:, :, None] * BLK + jnp.arange(BLK, dtype=jnp.int32)[None, None, :]
    ).reshape(q_heads, vert_count * BLK)
    want_window = first_row - 2 * row_count + jnp.arange(3 * row_count, dtype=jnp.int32)
    empty_vert = jnp.zeros((2, q_heads, vert_count * BLK, HD), jnp.bfloat16)
    empty_window = jnp.zeros((2, 3 * row_count, kv_heads, HD), jnp.bfloat16)
    piece_rows = lax.all_gather(kv_local, "qblk", axis=1, tiled=True)
    window = take_rows(piece_rows, want_window, empty_window)
    vert_rows = take_vertical(piece_rows, want_vert, kv_select, empty_vert)
    group_rows = min(512, row_count)
    group_blocks = group_rows // BLK
    front = 2 * row_count
    head_outputs = []
    for head_slot in range(q_heads):
        kv_slot = head_slot // (q_heads // kv_heads)
        k_window = window[0, :, kv_slot]
        v_window = window[1, :, kv_slot]
        q_head = q_local[0, :, head_slot]
        vertical_key_block = vert_rows[0, head_slot].reshape(vert_count, BLK, HD)
        vertical_value_block = vert_rows[1, head_slot].reshape(vert_count, BLK, HD)
        slash_row = slash_mine[head_slot]
        vert_row = vert_mine[head_slot]

        def one_group(group_index):
            start_row = group_index * group_rows
            query_block_list = lax.dynamic_slice_in_dim(q_head, start_row, group_rows, 0).reshape(
                group_blocks, BLK, HD
            )
            diagonal_key_block = lax.dynamic_slice_in_dim(
                k_window, front + start_row, group_rows, 0
            ).reshape(group_blocks, BLK, HD)
            diagonal_value_block = lax.dynamic_slice_in_dim(
                v_window, front + start_row, group_rows, 0
            ).reshape(group_blocks, BLK, HD)

            def slash_rows(source, offset_blocks):
                return lax.dynamic_slice_in_dim(
                    source, front + start_row - offset_blocks * BLK, group_rows, 0
                )

            slash_key_block = jax.vmap(slash_rows, in_axes=(None, 0))(k_window, slash_row).reshape(
                slash_count, group_blocks, BLK, HD
            )
            slash_value_block = jax.vmap(slash_rows, in_axes=(None, 0))(
                v_window, slash_row
            ).reshape(slash_count, group_blocks, BLK, HD)
            block_ids = (
                block_index * (row_count // BLK)
                + start_row // BLK
                + jnp.arange(group_blocks, dtype=jnp.int32)
            )
            return attend_group(
                query_block_list,
                diagonal_key_block,
                diagonal_value_block,
                slash_key_block,
                slash_value_block,
                vertical_key_block,
                vertical_value_block,
                block_ids,
                slash_row,
                vert_row,
            )

        grouped = lax.map(one_group, jnp.arange(row_count // group_rows, dtype=jnp.int32))
        head_outputs.append(grouped.reshape(row_count, HD))
    stacked = jnp.stack(head_outputs, axis=1)
    returned = lax.all_to_all(stacked, "head", split_axis=0, concat_axis=1, tiled=True)
    return returned.reshape(returned.shape[0], H * HD)


def solution(mesh):
    return jax.shard_map(
        per_device,
        mesh=mesh,
        in_specs=(
            P(("qblk", "head"), None),
            P(("qblk", "head"), None),
            P(("qblk", "head"), None),
            P(),
            P(),
        ),
        out_specs=P(("qblk", "head"), None),
        check_vma=False,
    )
```

profile of v0, /device:TPU:1, one launch (start us, length us, event | category | flops | bytes accessed | tf_op | source)
XLA Modules:
  0.0 659.2 jit_solution(17344250454945235806)
XLA Ops:
  9.0 23.3 %all_to_all.51 = bf16[2,128,16,128]{3,1,0,2:T(8,128)(2,1)S(1)} all-to-all(bf16[2,128,16,128]{3,1,0,2:T(8,128)(2,1)S(1)} %bitcast.250), channel_id=1, replica_groups=mesh['head'=16,'qblk'=16] {'head'}, dimensions={2} | all-to-all | bytes 2097152 | tf_op jit(solution)/shard_map/all_to_all | solution.py:122
  48.2 13.6 %all-to-all-done = bf16[1,128,32,128]{1,3,0,2:T(8,128)(2,1)S(1)} async-done(((bf16[1,128,32,128]{1,3,0,2:T(8,128)(2,1)}), bf16[1,128,32,128]{1,3,0,2:T(8,128)(2,1)S(1)}, u32[]{:S(2)}, u32[]{:S(2)}) %all-to-all-start) | async-done | bytes 1048608 | tf_op jit(solution)/shard_map/all_to_all | solution.py:121
  63.6 75.2 %all-gather.2.cloned.1.call-done = bf16[2,32768,1,128]{3,0,2,1:T(2,128)(2,1)} async-done(((bf16[2,2048,1,128]{3,0,2,1:T(2,128)(2,1)}), bf16[2,32768,1,128]{3,0,2,1:T(2,128)(2,1)}) %all-gather.2.cloned.1.call-update) | async-done | bytes 16777232 | tf_op jit(solution)/shard_map/all_gather | solution.py:137
  148.8 45.8 %gather_fusion = bf16[6144,2,128]{2,1,0:T(2,128)(2,1)} fusion(bf16[2,32768,128]{2,0,1:T(2,128)(2,1)} %bitcast.263, s32[6144]{0:T(1024)S(1)} %broadcast_clamp_fusion), kind=kCustom, calls=%fused_computation | custom fusion | bytes 6316032 | tf_op jit(solution)/shard_map/jit(_take)/gather | solution.py:98
  194.6 27.9 %broadcast_select_fusion.1 = bf16[2,6144,1,128]{3,0,1,2:T(2,128)(2,1)S(1)} fusion(pred[6144]{0:T(1024)(128)(4,1)S(1)} %get-tuple-element.454, bf16[6144,2,128]{2,1,0:T(2,128)(2,1)} %gather_fusion, pred[6144]{0:T(1024)(128)(4,1)S(1)} %get-tuple-element.453), kind=kLoop, calls=%fused_computation.107 | loop fusion | flops 3145728 | bytes 6303744 | tf_op jit(solution)/shard_map/jit(_where)/select_n | solution.py:99
  229.5 199.8 %while.34 = (s32[]{:T(128)}, bf16[4,8,64,128]{3,2,1,0:T(8,128)(2,1)}, s32[4]{0:T(128)S(1)}, bf16[2048,128]{1,0:T(8,128)(2,1)}, bf16[6144,128]{1,0:T(8,128)(2,1)}...) while((s32[]{:T(128)}, ...), condition=%wide.region_8.9_spmd, body=%wide.region_0.8_spmd.sunk | while | flops 239407072 | bytes 13391324 | solution.py:195
  231.9 18.7 %while.38 = (s32[]{:T(128)}, bf16[6144,128]{1,0:T(8,128)(2,1)}, s32[8,2]{0,1:T(2,128)S(1)}, bf16[8,512,128]{2,1,0:T(8,128)(2,1)S(1)}, s32[]{:T(128)}) while((s32[]{:T(128)}, bf16[6144,128]{1,0:T(8,128)(2,1)}, s32[8,2]{0,1:T(2,128)S(1)}, bf16[8,512,128]{2,1,0:T(8,128)(2,1)S(1)}, s32[]{:T(128)}) %tuple.145), condition=%wide.while_cond, body=%wide.while_body.sunk | while | flops 2 | bytes 262241 | solution.py:167
  259.0 16.4 %while.39 = (s32[]{:T(128)}, bf16[6144,128]{1,0:T(8,128)(2,1)S(1)}, s32[8,2]{0,1:T(2,128)S(1)}, bf16[8,512,128]{2,1,0:T(8,128)(2,1)}, s32[]{:T(128)}) while((s32[]{:T(128)}, bf16[6144,128]{1,0:T(8,128)(2,1)S(1)}, s32[8,2]{0,1:T(2,128)S(1)}, bf16[8,512,128]{2,1,0:T(8,128)(2,1)}, s32[]{:T(128)}) %tuple.161), condition=%wide.while_cond.1, body=%wide.while_body.1.sunk | while | flops 2 | bytes 263257 | solution.py:167
  281.9 18.7 %while.38 = (s32[]{:T(128)}, bf16[6144,128]{1,0:T(8,128)(2,1)}, s32[8,2]{0,1:T(2,128)S(1)}, bf16[8,512,128]{2,1,0:T(8,128)(2,1)S(1)}, s32[]{:T(128)}) while((s32[]{:T(128)}, bf16[6144,128]{1,0:T(8,128)(2,1)}, s32[8,2]{0,1:T(2,128)S(1)}, bf16[8,512,128]{2,1,0:T(8,128)(2,1)S(1)}, s32[]{:T(128)}) %tuple.145), condition=%wide.while_cond, body=%wide.while_body.sunk | while | flops 2 | bytes 262241 | solution.py:167
  308.9 16.4 %while.39 = (s32[]{:T(128)}, bf16[6144,128]{1,0:T(8,128)(2,1)S(1)}, s32[8,2]{0,1:T(2,128)S(1)}, bf16[8,512,128]{2,1,0:T(8,128)(2,1)}, s32[]{:T(128)}) while((s32[]{:T(128)}, bf16[6144,128]{1,0:T(8,128)(2,1)S(1)}, s32[8,2]{0,1:T(2,128)S(1)}, bf16[8,512,128]{2,1,0:T(8,128)(2,1)}, s32[]{:T(128)}) %tuple.161), condition=%wide.while_cond.1, body=%wide.while_body.1.sunk | while | flops 2 | bytes 263257 | solution.py:167
  331.8 18.7 %while.38 = (s32[]{:T(128)}, bf16[6144,128]{1,0:T(8,128)(2,1)}, s32[8,2]{0,1:T(2,128)S(1)}, bf16[8,512,128]{2,1,0:T(8,128)(2,1)S(1)}, s32[]{:T(128)}) while((s32[]{:T(128)}, bf16[6144,128]{1,0:T(8,128)(2,1)}, s32[8,2]{0,1:T(2,128)S(1)}, bf16[8,512,128]{2,1,0:T(8,128)(2,1)S(1)}, s32[]{:T(128)}) %tuple.145), condition=%wide.while_cond, body=%wide.while_body.sunk | while | flops 2 | bytes 262241 | solution.py:167
  358.9 16.4 %while.39 = (s32[]{:T(128)}, bf16[6144,128]{1,0:T(8,128)(2,1)S(1)}, s32[8,2]{0,1:T(2,128)S(1)}, bf16[8,512,128]{2,1,0:T(8,128)(2,1)}, s32[]{:T(128)}) while((s32[]{:T(128)}, bf16[6144,128]{1,0:T(8,128)(2,1)S(1)}, s32[8,2]{0,1:T(2,128)S(1)}, bf16[8,512,128]{2,1,0:T(8,128)(2,1)}, s32[]{:T(128)}) %tuple.161), condition=%wide.while_cond.1, body=%wide.while_body.1.sunk | while | flops 2 | bytes 263257 | solution.py:167
  381.7 18.7 %while.38 = (s32[]{:T(128)}, bf16[6144,128]{1,0:T(8,128)(2,1)}, s32[8,2]{0,1:T(2,128)S(1)}, bf16[8,512,128]{2,1,0:T(8,128)(2,1)S(1)}, s32[]{:T(128)}) while((s32[]{:T(128)}, bf16[6144,128]{1,0:T(8,128)(2,1)}, s32[8,2]{0,1:T(2,128)S(1)}, bf16[8,512,128]{2,1,0:T(8,128)(2,1)S(1)}, s32[]{:T(128)}) %tuple.145), condition=%wide.while_cond, body=%wide.while_body.sunk | while | flops 2 | bytes 262241 | solution.py:167
  408.8 16.4 %while.39 = (s32[]{:T(128)}, bf16[6144,128]{1,0:T(8,128)(2,1)S(1)}, s32[8,2]{0,1:T(2,128)S(1)}, bf16[8,512,128]{2,1,0:T(8,128)(2,1)}, s32[]{:T(128)}) while((s32[]{:T(128)}, bf16[6144,128]{1,0:T(8,128)(2,1)S(1)}, s32[8,2]{0,1:T(2,128)S(1)}, bf16[8,512,128]{2,1,0:T(8,128)(2,1)}, s32[]{:T(128)}) %tuple.161), condition=%wide.while_cond.1, body=%wide.while_body.1.sunk | while | flops 2 | bytes 263257 | solution.py:167
  430.2 187.7 %while.37 = (s32[]{:T(128)}, bf16[4,8,64,128]{3,2,1,0:T(8,128)(2,1)}, s32[4]{0:T(128)S(1)}, bf16[2048,128]{1,0:T(8,128)(2,1)}, bf16[6144,128]{1,0:T(8,128)(2,1)}...) while((s32[]{:T(128)}, ...), condition=%wide.region_17.18_spmd, body=%wide.region_9.17_spmd.sunk | while | flops 239407072 | bytes 13391324 | solution.py:195
  432.7 17.6 %while.40 = (s32[]{:T(128)}, bf16[6144,128]{1,0:T(8,128)(2,1)}, s32[8,2]{0,1:T(2,128)S(1)}, bf16[8,512,128]{2,1,0:T(8,128)(2,1)S(1)}, s32[]{:T(128)}) while((s32[]{:T(128)}, bf16[6144,128]{1,0:T(8,128)(2,1)}, s32[8,2]{0,1:T(2,128)S(1)}, bf16[8,512,128]{2,1,0:T(8,128)(2,1)S(1)}, s32[]{:T(128)}) %tuple.139), condition=%wide.while_cond.2, body=%wide.while_body.2.sunk | while | flops 2 | bytes 262241 | solution.py:167
  457.8 15.4 %while.41 = (s32[]{:T(128)}, bf16[6144,128]{1,0:T(8,128)(2,1)S(1)}, s32[8,2]{0,1:T(2,128)S(1)}, bf16[8,512,128]{2,1,0:T(8,128)(2,1)}, s32[]{:T(128)}) while((s32[]{:T(128)}, bf16[6144,128]{1,0:T(8,128)(2,1)S(1)}, s32[8,2]{0,1:T(2,128)S(1)}, bf16[8,512,128]{2,1,0:T(8,128)(2,1)}, s32[]{:T(128)}) %tuple.162), condition=%wide.while_cond.3, body=%wide.while_body.3.sunk | while | flops 2 | bytes 263257 | solution.py:167
  479.6 17.6 %while.40 = (s32[]{:T(128)}, bf16[6144,128]{1,0:T(8,128)(2,1)}, s32[8,2]{0,1:T(2,128)S(1)}, bf16[8,512,128]{2,1,0:T(8,128)(2,1)S(1)}, s32[]{:T(128)}) while((s32[]{:T(128)}, bf16[6144,128]{1,0:T(8,128)(2,1)}, s32[8,2]{0,1:T(2,128)S(1)}, bf16[8,512,128]{2,1,0:T(8,128)(2,1)S(1)}, s32[]{:T(128)}) %tuple.139), condition=%wide.while_cond.2, body=%wide.while_body.2.sunk | while | flops 2 | bytes 262241 | solution.py:167
  504.7 15.4 %while.41 = (s32[]{:T(128)}, bf16[6144,128]{1,0:T(8,128)(2,1)S(1)}, s32[8,2]{0,1:T(2,128)S(1)}, bf16[8,512,128]{2,1,0:T(8,128)(2,1)}, s32[]{:T(128)}) while((s32[]{:T(128)}, bf16[6144,128]{1,0:T(8,128)(2,1)S(1)}, s32[8,2]{0,1:T(2,128)S(1)}, bf16[8,512,128]{2,1,0:T(8,128)(2,1)}, s32[]{:T(128)}) %tuple.162), condition=%wide.while_cond.3, body=%wide.while_body.3.sunk | while | flops 2 | bytes 263257 | solution.py:167
  526.5 17.6 %while.40 = (s32[]{:T(128)}, bf16[6144,128]{1,0:T(8,128)(2,1)}, s32[8,2]{0,1:T(2,128)S(1)}, bf16[8,512,128]{2,1,0:T(8,128)(2,1)S(1)}, s32[]{:T(128)}) while((s32[]{:T(128)}, bf16[6144,128]{1,0:T(8,128)(2,1)}, s32[8,2]{0,1:T(2,128)S(1)}, bf16[8,512,128]{2,1,0:T(8,128)(2,1)S(1)}, s32[]{:T(128)}) %tuple.139), condition=%wide.while_cond.2, body=%wide.while_body.2.sunk | while | flops 2 | bytes 262241 | solution.py:167
  551.6 15.4 %while.41 = (s32[]{:T(128)}, bf16[6144,128]{1,0:T(8,128)(2,1)S(1)}, s32[8,2]{0,1:T(2,128)S(1)}, bf16[8,512,128]{2,1,0:T(8,128)(2,1)}, s32[]{:T(128)}) while((s32[]{:T(128)}, bf16[6144,128]{1,0:T(8,128)(2,1)S(1)}, s32[8,2]{0,1:T(2,128)S(1)}, bf16[8,512,128]{2,1,0:T(8,128)(2,1)}, s32[]{:T(128)}) %tuple.162), condition=%wide.while_cond.3, body=%wide.while_body.3.sunk | while | flops 2 | bytes 263257 | solution.py:167
  573.4 17.6 %while.40 = (s32[]{:T(128)}, bf16[6144,128]{1,0:T(8,128)(2,1)}, s32[8,2]{0,1:T(2,128)S(1)}, bf16[8,512,128]{2,1,0:T(8,128)(2,1)S(1)}, s32[]{:T(128)}) while((s32[]{:T(128)}, bf16[6144,128]{1,0:T(8,128)(2,1)}, s32[8,2]{0,1:T(2,128)S(1)}, bf16[8,512,128]{2,1,0:T(8,128)(2,1)S(1)}, s32[]{:T(128)}) %tuple.139), condition=%wide.while_cond.2, body=%wide.while_body.2.sunk | while | flops 2 | bytes 262241 | solution.py:167
  598.5 15.4 %while.41 = (s32[]{:T(128)}, bf16[6144,128]{1,0:T(8,128)(2,1)S(1)}, s32[8,2]{0,1:T(2,128)S(1)}, bf16[8,512,128]{2,1,0:T(8,128)(2,1)}, s32[]{:T(128)}) while((s32[]{:T(128)}, bf16[6144,128]{1,0:T(8,128)(2,1)S(1)}, s32[8,2]{0,1:T(2,128)S(1)}, bf16[8,512,128]{2,1,0:T(8,128)(2,1)}, s32[]{:T(128)}) %tuple.162), condition=%wide.while_cond.3, body=%wide.while_body.3.sunk | while | flops 2 | bytes 263257 | solution.py:167
  627.9 22.3 %all_to_all.52 = bf16[2048,2,128]{2,1,0:T(2,128)(2,1)S(1)} all-to-all(bf16[2048,2,128]{2,1,0:T(2,128)(2,1)S(1)} %copy.131), channel_id=1, replica_groups=mesh['head'=16,'qblk'=16] {'head'}, dimensions={0} | all-to-all | bytes 2097152 | tf_op jit(solution)/shard_map/all_to_all | solution.py:198
  (655 shorter events, 429.8 us)
Async XLA Ops:
  6.5 41.2 %copy-start = (s32[32,8]{0,1:T(8,128)S(1)}, s32[32,8]{0,1:T(8,128)}, u32[]{:S(2)}) copy-start(s32[32,8]{0,1:T(8,128)} %param.13) | copy-start | bytes 3076
  6.5 132.3 %all-gather.2.cloned.1.call-start = ((), (), s32[]{:S(2)}) async-start(), calls=%async_computation.3 | async-start | bytes 17825792 | tf_op jit(solution)/shard_map/all_gather | solution.py:137
  32.4 9.5 %copy-start.3 = (bf16[128,4096]{1,0:T(8,128)(2,1)S(1)}, bf16[128,4096]{1,0:T(8,128)(2,1)}, u32[]{:S(2)}) copy-start(bf16[128,4096]{1,0:T(8,128)(2,1)} %param.9) | copy-start | bytes 3145732
  41.9 5.2 copy-start.4
  43.2 18.6 %all-to-all-start = ((bf16[1,128,32,128]{1,3,0,2:T(8,128)(2,1)}), bf16[1,128,32,128]{1,3,0,2:T(8,128)(2,1)S(1)}, u32[]{:S(2)}, u32[]{:S(2)}) async-start(bf16[1,128,32,128]{1,3,0,2:T(8,128)(2,1)} %bitcast.41), calls=%async_computation | async-start | bytes 2097152 | tf_op jit(solution)/shard_map/all_to_all | solution.py:121
  275.4 2.7 copy-start.1
  325.4 2.7 copy-start.1
  375.3 2.7 copy-start.1
  425.3 2.7 copy-start.1
  432.7 20.0 %copy-start.2 = (bf16[5,64,128]{2,1,0:T(8,128)(2,1)S(1)}, bf16[5,64,128]{2,1,0:T(8,128)(2,1)}, u32[]{:S(2)}) copy-start(bf16[5,64,128]{2,1,0:T(8,128)(2,1)} %get-tuple-element.892) | copy-start | bytes 245764 | tf_op jit(solution)/shard_map/while
  479.6 20.0 %copy-start.2 = (bf16[5,64,128]{2,1,0:T(8,128)(2,1)S(1)}, bf16[5,64,128]{2,1,0:T(8,128)(2,1)}, u32[]{:S(2)}) copy-start(bf16[5,64,128]{2,1,0:T(8,128)(2,1)} %get-tuple-element.892) | copy-start | bytes 245764 | tf_op jit(solution)/shard_map/while
  526.5 20.0 %copy-start.2 = (bf16[5,64,128]{2,1,0:T(8,128)(2,1)S(1)}, bf16[5,64,128]{2,1,0:T(8,128)(2,1)}, u32[]{:S(2)}) copy-start(bf16[5,64,128]{2,1,0:T(8,128)(2,1)} %get-tuple-element.892) | copy-start | bytes 245764 | tf_op jit(solution)/shard_map/while
  573.4 20.0 %copy-start.2 = (bf16[5,64,128]{2,1,0:T(8,128)(2,1)S(1)}, bf16[5,64,128]{2,1,0:T(8,128)(2,1)}, u32[]{:S(2)}) copy-start(bf16[5,64,128]{2,1,0:T(8,128)(2,1)} %get-tuple-element.892) | copy-start | bytes 245764 | tf_op jit(solution)/shard_map/while
Sparse Core Ops, SparseCore 0:
  42.0 96.7 all-gather.1
where the time goes:
time: 663 us; the launch traced here: 659 us
  local copies, waits for them, and re-layouts  392 us (59%)
  waiting for transfers between devices  88.8 us (13%)
  matrix products  54.3 us (8%)
  other arithmetic  53.4 us (8%)
  blocking collectives  45.6 us (7%)
  between operations  13.6 us (2%)
  loops' own time  7.63 us (1%)
    gather x384, local copies, waits for them, and re-layouts  272 us
    all_gather x1, waiting for transfers between devices, per_device(): piece_rows = lax.all_gather(kv_local, 'qblk', axis=1, tiled=True)  75.2 us
    gather x1, local copies, waits for them, and re-layouts, take_rows(): picked = jnp.take(piece_rows, jnp.clip(wanted, 0, count - 1), axis=1)  45.8 us
    select_n x1, other arithmetic, take_rows(): return jnp.where(inside[None, :, None, None], picked, current)  27.9 us
    all_to_all x1, blocking collectives, per_device(): lax.all_to_all(kv_pair, 'head', split_axis=2, concat_axis=1, tiled=True)  23.3 us
    all_to_all x1, blocking collectives, per_device(): lax.all_to_all(stacked, 'head', split_axis=0, concat_axis=1, tiled=True)  22.3 us
    dot_general x8, matrix products, attend_group(): jnp.einsum('mnop,ompj->mnj', slash_weights.astype(jnp.bfloat16), slash_va...  21.7 us
    reduce_sum x8, other arithmetic, attend_group(): jnp.sum(slash_weights, axis=(2, 3))  17.5 us
  transfers between devices with their start and end apart: 2, of which 2 were waited for; matrix products, arithmetic and copies ran while one was open for 1% of the time, Pallas kernels for 0%

commit v1 on v0

--- a/solution.py
+++ b/solution.py
@@ -7,6 +7,13 @@
 KVH = 8
 HD = 128
 BLK = 64
+
+
+def gather_over(x, axis, dim):
+    count = lax.axis_size(axis)
+    shards = jnp.stack([x for _ in range(count)])
+    shards = lax.all_to_all(shards, axis, split_axis=0, concat_axis=0)
+    return jnp.concatenate(shards, axis=dim)
 
 
 def attend_group(
@@ -134,7 +141,7 @@
     want_window = first_row - 2 * row_count + jnp.arange(3 * row_count, dtype=jnp.int32)
     empty_vert = jnp.zeros((2, q_heads, vert_count * BLK, HD), jnp.bfloat16)
     empty_window = jnp.zeros((2, 3 * row_count, kv_heads, HD), jnp.bfloat16)
-    piece_rows = lax.all_gather(kv_local, "qblk", axis=1, tiled=True)
+    piece_rows = gather_over(kv_local, "qblk", 1)
     window = take_rows(piece_rows, want_window, empty_window)
     vert_rows = take_vertical(piece_rows, want_vert, kv_select, empty_vert)
     group_rows = min(512, row_count)

time: 663 us -> 1120 us (1.69)
  waiting for transfers between devices: 88.8 us -> 386 us
  local copies, waits for them, and re-layouts: 392 us -> 574 us
  blocking collectives: 45.6 us -> 19 us
  starting transfers between devices: 3.84 us -> 23.7 us
  between operations: 13.6 us -> 0.22 us
    all_to_all x0 -> x2, waiting for transfers between devices: none -> 373 us  [the longest x1 358 us: gather_over(): shards = lax.all_to_all(shards, axis, split_axis=0, concat_axis=0)]
    reshape x0 -> x2, local copies, waits for them, and re-layouts: none -> 170 us  [gather_over(): return jnp.concatenate(shards, axis=dim)]
    all_gather x1 -> x0, waiting for transfers between devices: 75.2 us -> none  [per_device(): piece_rows = lax.all_gather(kv_local, 'qblk', axis=1, tiled=True)]
    all_to_all x1 -> x0, blocking collectives: 23.3 us -> none  [per_device(): lax.all_to_all(kv_pair, 'head', split_axis=2, concat_axis=1, tiled=True)]
    all_to_all x0 -> x2, starting transfers between devices: none -> 19.8 us  [the longest x1 12.2 us: gather_over(): shards = lax.all_to_all(shards, axis, split_axis=0, concat_axis=0)]
  transfers between devices with their start and end apart: 2 -> 3, of which waited for: 2 -> 3; matrix products, arithmetic and copies ran while one was open for 1% -> 1% of each run, Pallas kernels for 0% -> 0%
where the time goes in v1:
time: 1120 us
  local copies, waits for them, and re-layouts  574 us (51%)
  waiting for transfers between devices  386 us (34%)
  matrix products  54.3 us (5%)
  other arithmetic  53.4 us (5%)
  starting transfers between devices  23.7 us (2%)
  blocking collectives  19 us (2%)
    all_to_all x1, waiting for transfers between devices, gather_over(): shards = lax.all_to_all(shards, axis, split_axis=0, concat_axis=0)  358 us
    gather x384, local copies, waits for them, and re-layouts  267 us
    reshape x2, local copies, waits for them, and re-layouts, gather_over(): return jnp.concatenate(shards, axis=dim)  170 us
    gather x1, local copies, waits for them, and re-layouts, take_rows(): picked = jnp.take(piece_rows, jnp.clip(wanted, 0, count - 1), axis=1)  45.8 us
    select_n x1, other arithmetic, take_rows(): return jnp.where(inside[None, :, None, None], picked, current)  27.9 us
  transfers between devices with their start and end apart: 3, of which 3 were waited for; matrix products, arithmetic and copies ran while one was open for 1% of the time, Pallas kernels for 0%

profile of v1, /device:TPU:1, one launch (start us, length us, event | category | flops | bytes accessed | tf_op | source)
XLA Modules:
  0.0 1117.7 jit_solution(13644416961321729876)
XLA Ops:
  69.1 358.3 %all-to-all-done.2 = bf16[16,2,2048,1,128]{4,2,1,3,0:T(8,128)(2,1)} async-done(((bf16[16,2,2048,1,128]{4,2,1,3,0:T(8,128)(2,1)}), bf16[16,2,2048,1,128]{4,2,1,3,0:T(8,128)(2,1)}, u32[]{:S(2)}, u32[]{:S(2)}) %all-to-all-start.2) | async-done | bytes 16777248 | tf_op jit(solution)/shard_map/all_to_all | solution.py:15
  441.1 139.4 %copy.127 = bf16[2,32768,1,128]{3,0,2,1:T(2,128)(2,1)} copy(bf16[2,32768,1,128]{3,1,0,2:T(8,128)(2,1)S(1)} %bitcast.240) | data formatting | bytes 33554432 | tf_op jit(solution)/shard_map/reshape | solution.py:16
  590.5 30.9 %copy.124 = bf16[2,32768,128]{2,0,1:T(2,128)(2,1)} copy(bf16[2,32768,128]{2,1,0:T(8,128)(2,1)} %bitcast.241) | data formatting | bytes 33554432 | tf_op jit(solution)/shard_map/reshape | solution.py:16
  621.5 45.8 %gather_fusion = bf16[6144,2,128]{2,1,0:T(2,128)(2,1)} fusion(bf16[2,32768,128]{2,0,1:T(2,128)(2,1)} %copy.124, s32[6144]{0:T(1024)S(1)} %broadcast_clamp_fusion), kind=kCustom, calls=%fused_computation | custom fusion | bytes 6316032 | tf_op jit(solution)/shard_map/jit(_take)/gather | solution.py:105
  667.3 27.9 %broadcast_select_fusion.1 = bf16[2,6144,1,128]{3,0,1,2:T(2,128)(2,1)S(1)} fusion(pred[6144]{0:T(1024)(128)(4,1)S(1)} %get-tuple-element.454, bf16[6144,2,128]{2,1,0:T(2,128)(2,1)} %gather_fusion, pred[6144]{0:T(1024)(128)(4,1)S(1)} %get-tuple-element.453), kind=kLoop, calls=%fused_computation.107 | loop fusion | flops 3145728 | bytes 6303744 | tf_op jit(solution)/shard_map/jit(_where)/select_n | solution.py:106
  702.1 199.8 %while.34 = (s32[]{:T(128)}, bf16[4,8,64,128]{3,2,1,0:T(8,128)(2,1)}, s32[4]{0:T(128)S(1)}, bf16[2048,128]{1,0:T(8,128)(2,1)}, bf16[6144,128]{1,0:T(8,128)(2,1)}...) while((s32[]{:T(128)}, ...), condition=%wide.region_8.9_spmd, body=%wide.region_0.8_spmd.sunk | while | flops 239407072 | bytes 13391324 | solution.py:202
  704.5 18.7 %while.38 = (s32[]{:T(128)}, bf16[6144,128]{1,0:T(8,128)(2,1)}, s32[8,2]{0,1:T(2,128)S(1)}, bf16[8,512,128]{2,1,0:T(8,128)(2,1)S(1)}, s32[]{:T(128)}) while((s32[]{:T(128)}, bf16[6144,128]{1,0:T(8,128)(2,1)}, s32[8,2]{0,1:T(2,128)S(1)}, bf16[8,512,128]{2,1,0:T(8,128)(2,1)S(1)}, s32[]{:T(128)}) %tuple.145), condition=%wide.while_cond, body=%wide.while_body.sunk | while | flops 2 | bytes 262241 | solution.py:174
  731.6 16.4 %while.39 = (s32[]{:T(128)}, bf16[6144,128]{1,0:T(8,128)(2,1)S(1)}, s32[8,2]{0,1:T(2,128)S(1)}, bf16[8,512,128]{2,1,0:T(8,128)(2,1)}, s32[]{:T(128)}) while((s32[]{:T(128)}, bf16[6144,128]{1,0:T(8,128)(2,1)S(1)}, s32[8,2]{0,1:T(2,128)S(1)}, bf16[8,512,128]{2,1,0:T(8,128)(2,1)}, s32[]{:T(128)}) %tuple.159), condition=%wide.while_cond.1, body=%wide.while_body.1.sunk | while | flops 2 | bytes 263257 | solution.py:174
  754.5 18.7 %while.38 = (s32[]{:T(128)}, bf16[6144,128]{1,0:T(8,128)(2,1)}, s32[8,2]{0,1:T(2,128)S(1)}, bf16[8,512,128]{2,1,0:T(8,128)(2,1)S(1)}, s32[]{:T(128)}) while((s32[]{:T(128)}, bf16[6144,128]{1,0:T(8,128)(2,1)}, s32[8,2]{0,1:T(2,128)S(1)}, bf16[8,512,128]{2,1,0:T(8,128)(2,1)S(1)}, s32[]{:T(128)}) %tuple.145), condition=%wide.while_cond, body=%wide.while_body.sunk | while | flops 2 | bytes 262241 | solution.py:174
  781.6 16.4 %while.39 = (s32[]{:T(128)}, bf16[6144,128]{1,0:T(8,128)(2,1)S(1)}, s32[8,2]{0,1:T(2,128)S(1)}, bf16[8,512,128]{2,1,0:T(8,128)(2,1)}, s32[]{:T(128)}) while((s32[]{:T(128)}, bf16[6144,128]{1,0:T(8,128)(2,1)S(1)}, s32[8,2]{0,1:T(2,128)S(1)}, bf16[8,512,128]{2,1,0:T(8,128)(2,1)}, s32[]{:T(128)}) %tuple.159), condition=%wide.while_cond.1, body=%wide.while_body.1.sunk | while | flops 2 | bytes 263257 | solution.py:174
  804.4 18.7 %while.38 = (s32[]{:T(128)}, bf16[6144,128]{1,0:T(8,128)(2,1)}, s32[8,2]{0,1:T(2,128)S(1)}, bf16[8,512,128]{2,1,0:T(8,128)(2,1)S(1)}, s32[]{:T(128)}) while((s32[]{:T(128)}, bf16[6144,128]{1,0:T(8,128)(2,1)}, s32[8,2]{0,1:T(2,128)S(1)}, bf16[8,512,128]{2,1,0:T(8,128)(2,1)S(1)}, s32[]{:T(128)}) %tuple.145), condition=%wide.while_cond, body=%wide.while_body.sunk | while | flops 2 | bytes 262241 | solution.py:174
  831.5 16.4 %while.39 = (s32[]{:T(128)}, bf16[6144,128]{1,0:T(8,128)(2,1)S(1)}, s32[8,2]{0,1:T(2,128)S(1)}, bf16[8,512,128]{2,1,0:T(8,128)(2,1)}, s32[]{:T(128)}) while((s32[]{:T(128)}, bf16[6144,128]{1,0:T(8,128)(2,1)S(1)}, s32[8,2]{0,1:T(2,128)S(1)}, bf16[8,512,128]{2,1,0:T(8,128)(2,1)}, s32[]{:T(128)}) %tuple.159), condition=%wide.while_cond.1, body=%wide.while_body.1.sunk | while | flops 2 | bytes 263257 | solution.py:174
  854.4 18.7 %while.38 = (s32[]{:T(128)}, bf16[6144,128]{1,0:T(8,128)(2,1)}, s32[8,2]{0,1:T(2,128)S(1)}, bf16[8,512,128]{2,1,0:T(8,128)(2,1)S(1)}, s32[]{:T(128)}) while((s32[]{:T(128)}, bf16[6144,128]{1,0:T(8,128)(2,1)}, s32[8,2]{0,1:T(2,128)S(1)}, bf16[8,512,128]{2,1,0:T(8,128)(2,1)S(1)}, s32[]{:T(128)}) %tuple.145), condition=%wide.while_cond, body=%wide.while_body.sunk | while | flops 2 | bytes 262241 | solution.py:174
  881.5 16.4 %while.39 = (s32[]{:T(128)}, bf16[6144,128]{1,0:T(8,128)(2,1)S(1)}, s32[8,2]{0,1:T(2,128)S(1)}, bf16[8,512,128]{2,1,0:T(8,128)(2,1)}, s32[]{:T(128)}) while((s32[]{:T(128)}, bf16[6144,128]{1,0:T(8,128)(2,1)S(1)}, s32[8,2]{0,1:T(2,128)S(1)}, bf16[8,512,128]{2,1,0:T(8,128)(2,1)}, s32[]{:T(128)}) %tuple.159), condition=%wide.while_cond.1, body=%wide.while_body.1.sunk | while | flops 2 | bytes 263257 | solution.py:174
  902.8 183.5 %while.37 = (s32[]{:T(128)}, bf16[4,8,64,128]{3,2,1,0:T(8,128)(2,1)}, s32[4]{0:T(128)S(1)}, bf16[2048,128]{1,0:T(8,128)(2,1)}, bf16[6144,128]{1,0:T(8,128)(2,1)}...) while((s32[]{:T(128)}, ...), condition=%wide.region_17.18_spmd, body=%wide.region_9.17_spmd.sunk | while | flops 239407072 | bytes 13391324 | solution.py:202
  905.3 17.1 %while.40 = (s32[]{:T(128)}, bf16[6144,128]{1,0:T(8,128)(2,1)}, s32[8,2]{0,1:T(2,128)S(1)}, bf16[8,512,128]{2,1,0:T(8,128)(2,1)S(1)}, s32[]{:T(128)}) while((s32[]{:T(128)}, bf16[6144,128]{1,0:T(8,128)(2,1)}, s32[8,2]{0,1:T(2,128)S(1)}, bf16[8,512,128]{2,1,0:T(8,128)(2,1)S(1)}, s32[]{:T(128)}) %tuple.139), condition=%wide.while_cond.2, body=%wide.while_body.2.sunk | while | flops 2 | bytes 262241 | solution.py:174
  929.9 14.8 %while.41 = (s32[]{:T(128)}, bf16[6144,128]{1,0:T(8,128)(2,1)S(1)}, s32[8,2]{0,1:T(2,128)S(1)}, bf16[8,512,128]{2,1,0:T(8,128)(2,1)}, s32[]{:T(128)}) while((s32[]{:T(128)}, bf16[6144,128]{1,0:T(8,128)(2,1)S(1)}, s32[8,2]{0,1:T(2,128)S(1)}, bf16[8,512,128]{2,1,0:T(8,128)(2,1)}, s32[]{:T(128)}) %tuple.160), condition=%wide.while_cond.3, body=%wide.while_body.3.sunk | while | flops 2 | bytes 263257 | solution.py:174
  951.1 17.1 %while.40 = (s32[]{:T(128)}, bf16[6144,128]{1,0:T(8,128)(2,1)}, s32[8,2]{0,1:T(2,128)S(1)}, bf16[8,512,128]{2,1,0:T(8,128)(2,1)S(1)}, s32[]{:T(128)}) while((s32[]{:T(128)}, bf16[6144,128]{1,0:T(8,128)(2,1)}, s32[8,2]{0,1:T(2,128)S(1)}, bf16[8,512,128]{2,1,0:T(8,128)(2,1)S(1)}, s32[]{:T(128)}) %tuple.139), condition=%wide.while_cond.2, body=%wide.while_body.2.sunk | while | flops 2 | bytes 262241 | solution.py:174
  975.8 14.8 %while.41 = (s32[]{:T(128)}, bf16[6144,128]{1,0:T(8,128)(2,1)S(1)}, s32[8,2]{0,1:T(2,128)S(1)}, bf16[8,512,128]{2,1,0:T(8,128)(2,1)}, s32[]{:T(128)}) while((s32[]{:T(128)}, bf16[6144,128]{1,0:T(8,128)(2,1)S(1)}, s32[8,2]{0,1:T(2,128)S(1)}, bf16[8,512,128]{2,1,0:T(8,128)(2,1)}, s32[]{:T(128)}) %tuple.160), condition=%wide.while_cond.3, body=%wide.while_body.3.sunk | while | flops 2 | bytes 263257 | solution.py:174
  997.0 17.1 %while.40 = (s32[]{:T(128)}, bf16[6144,128]{1,0:T(8,128)(2,1)}, s32[8,2]{0,1:T(2,128)S(1)}, bf16[8,512,128]{2,1,0:T(8,128)(2,1)S(1)}, s32[]{:T(128)}) while((s32[]{:T(128)}, bf16[6144,128]{1,0:T(8,128)(2,1)}, s32[8,2]{0,1:T(2,128)S(1)}, bf16[8,512,128]{2,1,0:T(8,128)(2,1)S(1)}, s32[]{:T(128)}) %tuple.139), condition=%wide.while_cond.2, body=%wide.while_body.2.sunk | while | flops 2 | bytes 262241 | solution.py:174
  1021.6 14.8 %while.41 = (s32[]{:T(128)}, bf16[6144,128]{1,0:T(8,128)(2,1)S(1)}, s32[8,2]{0,1:T(2,128)S(1)}, bf16[8,512,128]{2,1,0:T(8,128)(2,1)}, s32[]{:T(128)}) while((s32[]{:T(128)}, bf16[6144,128]{1,0:T(8,128)(2,1)S(1)}, s32[8,2]{0,1:T(2,128)S(1)}, bf16[8,512,128]{2,1,0:T(8,128)(2,1)}, s32[]{:T(128)}) %tuple.160), condition=%wide.while_cond.3, body=%wide.while_body.3.sunk | while | flops 2 | bytes 263257 | solution.py:174
  1042.9 17.1 %while.40 = (s32[]{:T(128)}, bf16[6144,128]{1,0:T(8,128)(2,1)}, s32[8,2]{0,1:T(2,128)S(1)}, bf16[8,512,128]{2,1,0:T(8,128)(2,1)S(1)}, s32[]{:T(128)}) while((s32[]{:T(128)}, bf16[6144,128]{1,0:T(8,128)(2,1)}, s32[8,2]{0,1:T(2,128)S(1)}, bf16[8,512,128]{2,1,0:T(8,128)(2,1)S(1)}, s32[]{:T(128)}) %tuple.139), condition=%wide.while_cond.2, body=%wide.while_body.2.sunk | while | flops 2 | bytes 262241 | solution.py:174
  1067.5 14.8 %while.41 = (s32[]{:T(128)}, bf16[6144,128]{1,0:T(8,128)(2,1)S(1)}, s32[8,2]{0,1:T(2,128)S(1)}, bf16[8,512,128]{2,1,0:T(8,128)(2,1)}, s32[]{:T(128)}) while((s32[]{:T(128)}, bf16[6144,128]{1,0:T(8,128)(2,1)S(1)}, s32[8,2]{0,1:T(2,128)S(1)}, bf16[8,512,128]{2,1,0:T(8,128)(2,1)}, s32[]{:T(128)}) %tuple.160), condition=%wide.while_cond.3, body=%wide.while_body.3.sunk | while | flops 2 | bytes 263257 | solution.py:174
  1096.5 19.0 %all_to_all.53 = bf16[2048,2,128]{2,1,0:T(2,128)(2,1)S(1)} all-to-all(bf16[2048,2,128]{2,1,0:T(2,128)(2,1)S(1)} %copy.129), channel_id=1, replica_groups=mesh['head'=16,'qblk'=16] {'head'}, dimensions={0} | all-to-all | bytes 2097152 | tf_op jit(solution)/shard_map/all_to_all | solution.py:205
  (664 shorter events, 488.6 us)
Async XLA Ops:
  0.0 65.0 %copy-start = (s32[32,8]{0,1:T(8,128)S(1)}, s32[32,8]{0,1:T(8,128)}, u32[]{:S(2)}) copy-start(s32[32,8]{0,1:T(8,128)} %param.13) | copy-start | bytes 3076
  2.2 8.8 copy-start.6
  3.4 23.2 %all-to-all-start.1 = ((bf16[2,128,16,128]{3,1,0,2:T(8,128)(2,1)}), bf16[2,128,16,128]{3,1,0,2:T(8,128)(2,1)S(1)}, u32[]{:S(2)}, u32[]{:S(2)}) async-start(bf16[2,128,16,128]{3,1,0,2:T(8,128)(2,1)} %bitcast.46), calls=%async_computation.1 | async-start | bytes 2097152 | tf_op jit(solution)/shard_map/all_to_all | solution.py:129
  26.7 1.0 copy-start.3
  27.7 18.4 %all-to-all-start = ((bf16[1,128,32,128]{1,3,0,2:T(8,128)(2,1)}), bf16[1,128,32,128]{1,3,0,2:T(8,128)(2,1)S(1)}, u32[]{:S(2)}, u32[]{:S(2)}) async-start(bf16[1,128,32,128]{1,3,0,2:T(8,128)(2,1)} %bitcast.256), calls=%async_computation | async-start | bytes 2097152 | tf_op jit(solution)/shard_map/all_to_all | solution.py:128
  52.1 12.2 %copy-start.7 = (s32[32,5]{0,1:T(8,128)S(1)}, s32[32,5]{0,1:T(8,128)}, u32[]{:S(2)}) copy-start(s32[32,5]{0,1:T(8,128)} %param.12) | copy-start | bytes 1924
  52.1 375.3 %all-to-all-start.2 = ((bf16[16,2,2048,1,128]{4,2,1,3,0:T(8,128)(2,1)}), bf16[16,2,2048,1,128]{4,2,1,3,0:T(8,128)(2,1)}, u32[]{:S(2)}, u32[]{:S(2)}) async-start(bf16[16,2,2048,1,128]{4,2,1,3,0:T(8,128)(2,1)} %stack.16), calls=%async_computation.2 | async-start | bytes 33554432 | tf_op jit(solution)/shard_map/all_to_all | solution.py:15
  435.4 5.7 copy-start.2
  748.0 2.7 copy-start.4
  798.0 2.7 copy-start.4
  847.9 2.7 copy-start.4
  897.9 2.7 copy-start.4
  905.3 19.4 %copy-start.5 = (bf16[5,64,128]{2,1,0:T(8,128)(2,1)S(1)}, bf16[5,64,128]{2,1,0:T(8,128)(2,1)}, u32[]{:S(2)}) copy-start(bf16[5,64,128]{2,1,0:T(8,128)(2,1)} %get-tuple-element.892) | copy-start | bytes 245764 | tf_op jit(solution)/shard_map/while
  951.1 19.4 %copy-start.5 = (bf16[5,64,128]{2,1,0:T(8,128)(2,1)S(1)}, bf16[5,64,128]{2,1,0:T(8,128)(2,1)}, u32[]{:S(2)}) copy-start(bf16[5,64,128]{2,1,0:T(8,128)(2,1)} %get-tuple-element.892) | copy-start | bytes 245764 | tf_op jit(solution)/shard_map/while
  997.0 19.4 %copy-start.5 = (bf16[5,64,128]{2,1,0:T(8,128)(2,1)S(1)}, bf16[5,64,128]{2,1,0:T(8,128)(2,1)}, u32[]{:S(2)}) copy-start(bf16[5,64,128]{2,1,0:T(8,128)(2,1)} %get-tuple-element.892) | copy-start | bytes 245764 | tf_op jit(solution)/shard_map/while
  1042.9 19.4 %copy-start.5 = (bf16[5,64,128]{2,1,0:T(8,128)(2,1)S(1)}, bf16[5,64,128]{2,1,0:T(8,128)(2,1)}, u32[]{:S(2)}) copy-start(bf16[5,64,128]{2,1,0:T(8,128)(2,1)} %get-tuple-element.892) | copy-start | bytes 245764 | tf_op jit(solution)/shard_map/while
  1115.7 2.1 copy-start.1
